TPU v7x, 32 devices: a whole 2x2x4 slice. The times are simulated.
32 devices in a mesh: lat: 8 (over z, y), lon: 4 (over x, core).
Axes of the slice: x: 2, y: 2, z: 4, core: 2. Of those that a mesh axis runs over, the one named last changes fastest.
Arguments:
- state_fields: float32 [5, 32, 64, 4096], P(None, None, 'lat', 'lon'), may hold values from -6 to 6
- stencil_weights: float32 [4, 32, 64, 4096], P(None, None, 'lat', 'lon'), may hold values from 0.02 to 0.22
- filter_mask: int32 [64], replicated, may hold values from 0 to 1, as said below
- cutoff_wave: int32 [64], replicated, may hold values from 0 to 255, as said below
Outputs:
- advanced: float32 [5, 32, 64, 4096], P(None, None, 'lat', 'lon')
Inputs may be any that keep to these rules, and one draw needn't show every extreme that they name: `filter_mask`: every row outside the first and last 8 rows holds 0. `cutoff_wave`: from 1 to 255 in the first and last 8 rows, 0 elsewhere.
All inputs are finite; a program needn't handle non-finite values.
Results may differ from a plain program's by a relative error of at most 0.0011.
Values may be sent and summed in bfloat16 or wider, within the bound.
A program may use at most 64 MiB of HBM per device.

v0:
```python
import math

import jax
import jax.numpy as jnp
import numpy as np
from jax import lax
from jax.experimental import pallas as pl
from jax.experimental.pallas import tpu as pltpu
from jax.sharding import PartitionSpec as P

KC = 256


def angle_parts(columns, circle_size, axis):
    waves = lax.broadcasted_iota(
        jnp.int32, (columns.size, KC) if axis == 1 else (KC, columns.size), axis
    )
    product = jnp.expand_dims(columns, axis) * waves % circle_size
    angles = product.astype(jnp.float32) * (2.0 * math.pi / circle_size)
    return jnp.cos(angles), jnp.sin(angles)


MESH = pl.DeviceIdType.MESH


def step_kernel(
    state,
    weights,
    cosines,
    sines,
    turned_cosines,
    turned_sines,
    bounds,
    results,
    waves,
    turned,
    rounded,
    top,
    bottom,
    north,
    south,
    columns_out,
    columns_in,
    sides,
    partial,
    halves,
    quarters,
    half_in,
    quarter_in,
    spectra,
    row_send,
    row_recv,
    side_send,
    side_recv,
    sum_send,
    sum_recv,
    join_send,
    join_recv,
):
    fields, lines, columns = state.shape
    chunks, _, size, _ = top.shape
    depth = lines // chunks
    rows = depth // size
    modes = waves.shape[1] // 2
    half = partial.shape[1] // 2
    quarter = half // 2
    lat_count, lon_count = lax.axis_size("lat"), lax.axis_size("lon")
    lat, lon = lax.axis_index("lat"), lax.axis_index("lon")
    after = lax.rem(lon + 1, lon_count)
    before = lax.rem(lon + lon_count - 1, lon_count)
    across = lax.rem(lon + lon_count // 2, lon_count)
    bits = lon_count.bit_length() - 1
    digit = [lax.rem(lon // (1 << b), 2) for b in range(bits)]
    peer = [lon + (1 << b) - (2 << b) * digit[b] for b in range(bits)]
    own_half = digit[0] * half
    own_quarter = digit[1] * quarter

    def span_of(g, first, count):
        return pl.ds(pl.multiple_of(g * depth + first, count), count)

    def remote(source, target, sent, got, device):
        return pltpu.make_async_remote_copy(
            src_ref=source,
            dst_ref=target,
            send_sem=sent,
            recv_sem=got,
            device_id=device,
            device_id_type=MESH,
        )

    def row_copy(g, up, device, into_north):
        return remote(
            top.at[g] if up else bottom.at[g],
            north.at[g] if into_north else south.at[g],
            row_send.at[0 if up else 1, g],
            row_recv.at[0 if into_north else 1, g],
            device,
        )

    def side_copy(k, device):
        return remote(
            columns_out.at[k], columns_in.at[k], side_send.at[k], side_recv.at[k], device
        )

    def sum_copy(b, g):
        if b == 0:
            away = pl.ds(pl.multiple_of((1 - digit[0]) * half, 16), half)
            source, target = partial.at[g, away], half_in.at[g]
        elif b == 1:
            away = pl.ds(pl.multiple_of((1 - digit[1]) * quarter, 16), quarter)
            source, target = halves.at[g, away], quarter_in.at[0, g]
        else:
            source, target = quarters.at[b - 2, g], quarter_in.at[b - 1, g]
        return remote(source, target, sum_send.at[b, g], sum_recv.at[b, g], (lat, peer[b]))

    def join_copy(b, g):
        if b == 0:
            part = pl.ds(pl.multiple_of(own_half, 16), half)
        else:
            part = pl.ds(pl.multiple_of(own_half + own_quarter, 16), quarter)
        view = spectra.at[g, part]
        return remote(view, view, join_send.at[b, g], join_recv.at[b, g], (lat, peer[b]))

    barrier = pltpu.get_barrier_semaphore()
    for other in (after, before, across, *peer):
        pl.semaphore_signal(barrier, inc=1, device_id=(lat, other), device_id_type=MESH)

    @pl.when(lat > 0)
    def _():
        pl.semaphore_signal(barrier, inc=1, device_id=(lat - 1, lon), device_id_type=MESH)

    @pl.when(lat < lat_count - 1)
    def _():
        pl.semaphore_signal(barrier, inc=1, device_id=(lat + 1, lon), device_id_type=MESH)

    inside = (lat > 0) & (lat < lat_count - 1)

    @pl.when(inside)
    def _():
        pl.semaphore_wait(barrier, 5 + bits)

    @pl.when(jnp.logical_not(inside))
    def _():
        pl.semaphore_wait(barrier, 4 + bits)

    taker = lax.broadcasted_iota(jnp.int32, (2 * size, depth), 0)
    taken = lax.broadcasted_iota(jnp.int32, (2 * size, depth), 1)
    wanted = jnp.where(taker < size, taker * rows, (taker - size) * rows + rows - 1)
    gather = jnp.where(taken == wanted, 1.0, 0.0).astype(jnp.bfloat16)

    def send_rows(g, carry):
        for field in range(fields):
            sign = -1.0 if field < 2 else 1.0
            up_sign = jnp.where(lat == 0, sign, 1.0).astype(jnp.float32)
            down_sign = jnp.where(lat == lat_count - 1, sign, 1.0).astype(jnp.float32)
            edges = jnp.dot(
                gather,
                state[field, span_of(g, 0, depth)].astype(jnp.bfloat16),
                preferred_element_type=jnp.float32,
            )
            top[g, field] = (edges[:size] * up_sign).astype(jnp.bfloat16)
            bottom[g, field] = (edges[size:] * down_sign).astype(jnp.bfloat16)

        @pl.when(lat == 0)
        def _():
            row_copy(g, True, (lat, across), True).start()

        @pl.when(lat > 0)
        def _():
            row_copy(g, True, (lat - 1, lon), False).start()

        @pl.when(lat < lat_count - 1)
        def _():
            row_copy(g, False, (lat + 1, lon), True).start()

        @pl.when(lat == lat_count - 1)
        def _():
            row_copy(g, False, (lat, across), False).start()

        return carry

    lax.fori_loop(0, chunks, send_rows, 0)

    spot = lax.broadcasted_iota(jnp.int32, (16, 128), 1)
    line = lax.broadcasted_iota(jnp.int32, (16, 128), 0)

    def pick(k, lanes, lane):
        chosen = jnp.where((spot == lane) & (line == 0), 1.0, 0.0).astype(jnp.bfloat16)
        for g in range(chunks):
            for field in range(0, fields):
                first = (g * fields + field) * depth
                edge = state[field, span_of(g, 0, depth), lanes].astype(jnp.bfloat16)
                picked = lax.dot_general(
                    chosen, edge, (((1,), (1,)), ((), ())), preferred_element_type=jnp.float32
                )
                columns_out[k, g * fields + field] = picked.astype(jnp.bfloat16)

    pick(0, pl.ds(columns - 128, 128), 127)
    side_copy(0, (lat, after)).start()
    pick(1, pl.ds(0, 128), 0)
    side_copy(1, (lat, before)).start()

    fine = 32
    coarse = columns // fine
    fine_cos, fine_sin = cosines[coarse:], sines[coarse:]

    def fill(at, carry):
        span = pl.ds(pl.multiple_of(at * fine, fine), fine)
        coarse_cos, coarse_sin = cosines[pl.ds(at, 1)], sines[pl.ds(at, 1)]
        waves[span, :modes] = (coarse_cos * fine_cos - coarse_sin * fine_sin).astype(jnp.bfloat16)
        waves[span, modes:] = (coarse_sin * fine_cos + coarse_cos * fine_sin).astype(jnp.bfloat16)
        return carry

    lax.fori_loop(0, coarse, fill, 0)
    lane_cos, lane_sin = turned_cosines[:, :128], turned_sines[:, :128]
    for at in range(columns // 128):
        span = pl.ds(at * 128, 128)
        tile_cos = turned_cosines[:, 128 + at : 129 + at]
        tile_sin = turned_sines[:, 128 + at : 129 + at]
        turned[:modes, span] = (tile_cos * lane_cos - tile_sin * lane_sin).astype(jnp.bfloat16)
        turned[modes:, span] = (tile_sin * lane_cos + tile_cos * lane_sin).astype(jnp.bfloat16)

    spread = jnp.where(line == 0, 1.0, 0.0).astype(jnp.bfloat16)
    for k in range(2):
        side_copy(k, (lat, after)).wait_recv()
        for at in range(chunks * fields):
            sides[k, at] = lax.dot_general(
                columns_in[k, at],
                spread,
                (((0,), (0,)), ((), ())),
                preferred_element_type=jnp.float32,
            )

    lane = lax.broadcasted_iota(jnp.int32, (rows, columns), 1)
    level_line = lax.broadcasted_iota(jnp.int32, (rows, columns), 0)
    copies = columns // 128

    wave = lax.rem(lax.broadcasted_iota(jnp.int32, (rows, 2 * modes), 1), modes)
    circle_size = columns * lon_count
    weight = jnp.where(wave == 0, 1.0 / circle_size, 2.0 / circle_size)
    scale = jnp.where(wave <= bounds[:, 1:2], weight, 0.0).astype(jnp.float32)

    def advance(g):
        row_copy(g, True, (lat, across), True).wait_recv()
        row_copy(g, False, (lat, across), False).wait_recv()

        def one_field(field, inner):
            above = north[g, field].astype(jnp.float32)
            below = south[g, field].astype(jnp.float32)
            for level in range(0, size, 2):
                pair = []
                for at in (level, level + 1):
                    span = pl.ds(at * rows, rows)
                    here = span_of(g, at * rows, rows)
                    x = state[field, here]
                    left = jnp.concatenate([sides[0, g * fields + field, span]] * copies, axis=1)
                    right = jnp.concatenate([sides[1, g * fields + field, span]] * copies, axis=1)
                    w = jnp.where(lane == 0, left, pltpu.roll(x, 1, 1))
                    e = jnp.where(lane == columns - 1, right, pltpu.roll(x, columns - 1, 1))
                    n = jnp.where(level_line == 0, above[at : at + 1], pltpu.roll(x, 1, 0))
                    s = jnp.where(
                        level_line == rows - 1, below[at : at + 1], pltpu.roll(x, rows - 1, 0)
                    )
                    y = (
                        x
                        + weights[0, here] * (e - x)
                        + weights[1, here] * (w - x)
                        + weights[2, here] * (n - x)
                        + weights[3, here] * (s - x)
                    )
                    results[field, here] = y
                    pair.append(y)
                first = pl.multiple_of(field * depth + level * rows, 2 * rows)
                rounded[pl.ds(first, 2 * rows), :] = jnp.concatenate(pair, axis=0).astype(
                    jnp.bfloat16
                )
            return inner

        lax.fori_loop(0, fields, one_field, 0)
        partial[g] = jnp.dot(rounded[...], waves[...], preferred_element_type=jnp.float32)
        sum_copy(0, g).start()

    def pair_sum(g):
        sum_copy(0, g).wait_recv()
        mine = pl.ds(pl.multiple_of(own_half, 16), half)
        halves[g] = partial[g, mine] + half_in[g]
        sum_copy(1, g).start()

    def full_sum(g):
        sum_copy(1, g).wait_recv()
        mine = pl.ds(pl.multiple_of(own_quarter, 16), quarter)
        total = halves[g, mine] + quarter_in[0, g]
        for b in range(2, bits):
            quarters[b - 2, g] = total
            sum_copy(b, g).start()
            sum_copy(b, g).wait_recv()
            total = total + quarter_in[b - 1, g]
        scaled = total.reshape(quarter // rows, rows, 2 * modes) * scale[None]
        part = pl.ds(pl.multiple_of(own_half + own_quarter, 16), quarter)
        spectra[g, part] = scaled.reshape(quarter, 2 * modes).astype(jnp.bfloat16)
        join_copy(1, g).start()

    def join(g):
        join_copy(1, g).wait_recv()
        join_copy(0, g).start()

    def merge(g):
        join_copy(0, g).wait_recv()
        smooth = jnp.dot(spectra[g], turned[...], preferred_element_type=jnp.float32)
        smooth = smooth.astype(jnp.bfloat16).astype(jnp.float32)
        smooth = smooth.reshape(fields, size, rows, columns)
        kept = jnp.broadcast_to(bounds[:, 0:1], (rows, columns)) != 0
        for field in range(fields):
            for at in range(size):
                here = span_of(g, at * rows, rows)
                results[field, here] = jnp.where(kept, smooth[field, at], results[field, here])

    def forward(t, carry):
        advance(t)

        @pl.when(t >= 1)
        def _():
            pair_sum(t - 1)

        return carry

    last = chunks - 1
    lax.fori_loop(0, chunks, forward, 0)
    full_sum(0)
    pair_sum(last)

    def sums(g, carry):
        full_sum(g)
        return carry

    def joins(g, carry):
        join(g)
        return carry

    def merges(g, carry):
        merge(g)

        @pl.when(g + 2 < chunks)
        def _():
            join(g + 2)

        return carry

    lax.fori_loop(1, last, sums, 0)
    lax.fori_loop(0, 2, joins, 0)
    full_sum(last)
    lax.fori_loop(0, chunks, merges, 0)

    def finish(g, carry):
        for b in range(bits):
            sum_copy(b, g).wait_send()
        for b in range(2):
            join_copy(b, g).wait_send()
        row_copy(g, True, (lat, across), True).wait_send()
        row_copy(g, False, (lat, across), False).wait_send()
        return carry

    lax.fori_loop(0, chunks, finish, 0)
    for k in range(2):
        side_copy(k, (lat, after)).wait_send()


def on_device(state_fields, stencil_weights, filter_mask, cutoff_wave):
    fields, levels, rows, columns = state_fields.shape
    lat_count, lon_count = lax.axis_size("lat"), lax.axis_size("lon")
    lat_pos, lon_pos = lax.axis_index("lat"), lax.axis_index("lon")
    circle_size = columns * lon_count
    size = 8
    steps = levels // size
    start = lat_pos * rows
    bounds = lax.dynamic_slice_in_dim(jnp.stack([filter_mask, cutoff_wave], axis=1), start, rows)
    origin = lon_pos * columns
    cosines, sines = angle_parts(
        jnp.concatenate(
            [origin + 32 * jnp.arange(columns // 32), jnp.arange(32)]
        ).astype(jnp.int32),
        circle_size,
        1,
    )
    turned_cosines, turned_sines = angle_parts(
        jnp.concatenate(
            [jnp.arange(128), origin + 128 * jnp.arange(columns // 128)]
        ).astype(jnp.int32),
        circle_size,
        0,
    )
    rows_each = fields * size * rows
    depth = size * rows
    dma = pltpu.SemaphoreType.DMA
    strip = pltpu.VMEM((steps, fields, size, columns), jnp.bfloat16)
    column_strip = pltpu.VMEM((2, steps * fields, 16, depth), jnp.bfloat16)
    extra = max(lon_count.bit_length() - 3, 1)
    in_vmem = pl.BlockSpec(memory_space=pltpu.VMEM)
    bits = lon_count.bit_length() - 1
    advanced = pl.pallas_call(
        step_kernel,
        in_specs=[in_vmem] * 7,
        out_specs=in_vmem,
        out_shape=jax.ShapeDtypeStruct((fields, levels * rows, columns), jnp.float32),
        scratch_shapes=[
            pltpu.VMEM((columns, 2 * KC), jnp.bfloat16),
            pltpu.VMEM((2 * KC, columns), jnp.bfloat16),
            pltpu.VMEM((rows_each, columns), jnp.bfloat16),
            strip,
            strip,
            strip,
            strip,
            column_strip,
            column_strip,
            pltpu.VMEM((2, steps * fields, depth, 128), jnp.float32),
            pltpu.VMEM((steps, rows_each, 2 * KC), jnp.float32),
            pltpu.VMEM((steps, rows_each // 2, 2 * KC), jnp.float32),
            pltpu.VMEM((extra, steps, rows_each // 4, 2 * KC), jnp.float32),
            pltpu.VMEM((steps, rows_each // 2, 2 * KC), jnp.float32),
            pltpu.VMEM((bits - 1, steps, rows_each // 4, 2 * KC), jnp.float32),
            pltpu.VMEM((steps, rows_each, 2 * KC), jnp.bfloat16),
            dma((2, steps)),
            dma((2, steps)),
            dma((2,)),
            dma((2,)),
            dma((bits, steps)),
            dma((bits, steps)),
            dma((2, steps)),
            dma((2, steps)),
        ],
        compiler_params=pltpu.CompilerParams(
            collective_id=0, has_side_effects=True, vmem_limit_bytes=38 << 20
        ),
        name="step",
    )(
        state_fields.reshape(fields, levels * rows, columns),
        stencil_weights.reshape(4, levels * rows, columns),
        cosines,
        sines,
        turned_cosines,
        turned_sines,
        bounds,
    )
    return advanced.reshape(state_fields.shape)


def roots_table(columns, circle_size):
    steps = np.arange(columns)[:, None] * np.arange(KC)[None, :] % circle_size
    angles = steps * (2.0 * np.pi / circle_size)
    return np.concatenate([np.cos(angles), np.sin(angles)], axis=1).astype(jnp.bfloat16)


def quarter_turns(shape, axis, turns):
    phase = lax.rem(lax.broadcasted_iota(jnp.int32, shape, axis) * turns, 4)
    a = jnp.where(phase == 0, 1.0, jnp.where(phase == 2, -1.0, 0.0))
    b = jnp.where(phase == 1, 1.0, jnp.where(phase == 3, -1.0, 0.0))
    return a.astype(jnp.float32), b.astype(jnp.float32)


RELAYED = 4
FINISH = (0, 4, 1, 5, 2, 6, 3, 7)


def caps_kernel(
    state,
    weights,
    mask_in,
    cutoff_in,
    waves_in,
    turned_in,
    results,
    xs,
    ws,
    waves,
    turned,
    mask,
    cutoff,
    rounded,
    edges,
    halos,
    columns_out,
    columns_in,
    partial,
    half_in,
    coded,
    coded_in,
    passing,
    spectra,
    state_sem,
    weight_sem,
    table_sem,
    edge_send,
    edge_recv,
    column_send,
    column_recv,
    half_send,
    half_recv,
    code_send,
    code_recv,
    pass_send,
    pass_recv,
    join_send,
    join_recv,
):
    rows, fields, levels, columns = results.shape
    groups = levels // 8
    lines = fields * levels
    half = lines // 2
    lat_count, lon_count = lax.axis_size("lat"), lax.axis_size("lon")
    lat, lon = lax.axis_index("lat"), lax.axis_index("lon")
    after = lax.rem(lon + 1, lon_count)
    before = lax.rem(lon + lon_count - 1, lon_count)
    across = lax.rem(lon + lon_count // 2, lon_count)
    core = lax.rem(lon, 2)
    partner = lon + 1 - 2 * core
    circle_size = columns * lon_count
    first, last = lat == 0, lat == lat_count - 1
    polar = first | last
    middle = (lat == 2) | (lat == lat_count - 3)
    helper = jnp.where(first, 2, lat_count - 3)
    served = jnp.where(lat == 2, 0, lat_count - 1)
    edge_row = jnp.where(last, 0, rows - 1)

    def row_at(i):
        return jnp.where(i < rows - 2, i + 1, jnp.where(i == rows - 2, edge_row, rows - 1 - edge_row))

    own = pl.ds(pl.multiple_of(core * half, 16), half)
    other = pl.ds(pl.multiple_of((1 - core) * half, 16), half)

    def remote(source, target, sent, got, device):
        return pltpu.make_async_remote_copy(
            src_ref=source,
            dst_ref=target,
            send_sem=sent,
            recv_sem=got,
            device_id=device,
            device_id_type=MESH,
        )

    def state_copy(r):
        return pltpu.make_async_copy(state.at[:, :, r], xs.at[r + 1], state_sem.at[r])

    def weight_copy(r):
        return pltpu.make_async_copy(weights.at[:, :, r], ws.at[r], weight_sem.at[r])

    def table_copies():
        return (
            pltpu.make_async_copy(waves_in, waves, table_sem.at[0]),
            pltpu.make_async_copy(turned_in, turned, table_sem.at[1]),
        )

    def bound_copies():
        return (
            pltpu.make_async_copy(mask_in, mask, table_sem.at[2]),
            pltpu.make_async_copy(cutoff_in, cutoff, table_sem.at[3]),
        )

    def edge_copy(k, field, side, device):
        return remote(
            edges.at[k, field],
            halos.at[side, field],
            edge_send.at[k, field],
            edge_recv.at[side, field],
            device,
        )

    def column_copy(k, r, device):
        return remote(
            columns_out.at[k, r],
            columns_in.at[k, r],
            column_send.at[k, r],
            column_recv.at[k, r],
            device,
        )

    def half_copy(i):
        return remote(
            partial.at[i, other], half_in.at[i], half_send.at[i], half_recv.at[i], (lat, partner)
        )

    def code_copy(i):
        return remote(
            coded.at[i], coded_in.at[i], code_send.at[i], code_recv.at[i], (lat, across)
        )

    def lend_copy(i):
        return remote(
            coded.at[i], passing.at[i], code_send.at[i], pass_recv.at[i], (helper, across)
        )

    def pass_copy(i):
        return remote(
            passing.at[i], coded_in.at[i], pass_send.at[i], code_recv.at[i], (served, lon)
        )

    def join_copy(i):
        view = spectra.at[i, own]
        return remote(view, view, join_send.at[i], join_recv.at[i], (lat, partner))

    order = (0, rows - 1, *range(1, rows - 1))
    for r in order:
        state_copy(r).start()
    for copy in bound_copies():
        copy.start()
    for r in (*range(1, rows - 1), 0, rows - 1):
        weight_copy(r).start()

    @pl.when(polar)
    def _():
        for copy in table_copies():
            copy.start()

    barrier = pltpu.get_barrier_semaphore()

    def greet(a, b):
        pl.semaphore_signal(barrier, inc=1, device_id=(a, b), device_id_type=MESH)

    for b in (after, before, across):
        greet(lat, b)

    @pl.when(lat > 0)
    def _():
        greet(lat - 1, lon)

    @pl.when(lat < lat_count - 1)
    def _():
        greet(lat + 1, lon)

    @pl.when(polar)
    def _():
        greet(helper, lon)
        greet(helper, across)

    @pl.when(middle)
    def _():
        greet(served, lon)
        greet(served, across)

    for r in (0, rows - 1):
        state_copy(r).wait()
    for field in range(fields):
        sign = -1.0 if field < 2 else 1.0
        up_sign = jnp.where(first, sign, 1.0).astype(jnp.float32)
        down_sign = jnp.where(last, sign, 1.0).astype(jnp.float32)
        edges[0, field] = (xs[1, field] * up_sign).astype(jnp.bfloat16)
        edges[1, field] = (xs[rows, field] * down_sign).astype(jnp.bfloat16)

    @pl.when(polar)
    def _():
        pl.semaphore_wait(barrier, 3 + 1 + 2)

    @pl.when(middle)
    def _():
        pl.semaphore_wait(barrier, 3 + 2 + 2)

    @pl.when(jnp.logical_not(polar | middle))
    def _():
        pl.semaphore_wait(barrier, 3 + 2)

    for field in range(fields):

        @pl.when(lat > 0)
        def _():
            edge_copy(0, field, 1, (lat - 1, lon)).start()

        @pl.when(lat < lat_count - 1)
        def _():
            edge_copy(1, field, 0, (lat + 1, lon)).start()

    spot = lax.broadcasted_iota(jnp.int32, (8, 128), 1)

    def send_columns(r):
        to_after = jnp.zeros((8, 128), jnp.float32)
        to_before = jnp.zeros((8, 128), jnp.float32)
        for group in range(groups):
            for field in range(fields):
                at = group * fields + field
                span = pl.ds(group * 8, 8)
                right = xs[r + 1, field, span, pl.ds(columns - 128, 128)]
                left = xs[r + 1, field, span, pl.ds(0, 128)]
                to_after = jnp.where(spot == at, pltpu.roll(right, at + 1, 1), to_after)
                left = pltpu.roll(left, at, 1) if at else left
                to_before = jnp.where(spot == at, left, to_before)
        columns_out[0, r] = to_after
        columns_out[1, r] = to_before
        column_copy(0, r, (lat, after)).start()
        column_copy(1, r, (lat, before)).start()

    for j, r in enumerate((*range(1, rows - 1), rows - 1, 0)):
        if 0 < r < rows - 1:
            state_copy(r).wait()
        send_columns(r)
        if 1 <= j <= fields:

            @pl.when(first)
            def _():
                edge_copy(0, j - 1, 0, (lat, across)).start()

            @pl.when(last)
            def _():
                edge_copy(1, j - 1, 1, (lat, across)).start()

    for copy in bound_copies():
        copy.wait()

    @pl.when(polar)
    def _():
        for copy in table_copies():
            copy.wait()
        a, b = quarter_turns((16, KC), 1, lon)

        def turn_waves(t, carry):
            span = pl.ds(pl.multiple_of(t * 16, 16), 16)
            c = waves[span, :KC].astype(jnp.float32)
            s = waves[span, KC:].astype(jnp.float32)
            waves[span, :KC] = (a * c - b * s).astype(jnp.bfloat16)
            waves[span, KC:] = (a * s + b * c).astype(jnp.bfloat16)
            return carry

        lax.fori_loop(0, columns // 16, turn_waves, 0)
        u, v = quarter_turns((16, 128), 0, lon)

        def turn_back(t, carry):
            low = pl.ds(pl.multiple_of(t * 16, 16), 16)
            high = pl.ds(pl.multiple_of(KC + t * 16, 16), 16)
            for tile in range(columns // 128):
                lanes = pl.ds(tile * 128, 128)
                c = turned[low, lanes].astype(jnp.float32)
                s = turned[high, lanes].astype(jnp.float32)
                turned[low, lanes] = (u * c - v * s).astype(jnp.bfloat16)
                turned[high, lanes] = (u * s + v * c).astype(jnp.bfloat16)
            return carry

        lax.fori_loop(0, KC // 16, turn_back, 0)

    tiles = columns // 128

    def step(r):
        for group in range(groups):
            span = pl.ds(group * 8, 8)
            east_w, west_w, north_w, south_w = (ws[r, q, span] for q in range(4))
            for field in range(fields):
                at = group * fields + field
                x = xs[r + 1, field, span]
                n = xs[r, field, span]
                s = xs[r + 2, field, span]
                parts = [x[:, t * 128 : t * 128 + 128] for t in range(tiles)]
                left = columns_in[0, r]
                left = pltpu.roll(left, 128 - at, 1) if at else left
                right = pltpu.roll(columns_in[1, r], 127 - at, 1)
                right_turned = [left] + [pltpu.roll(p, 1, 1) for p in parts]
                left_turned = [pltpu.roll(p, 127, 1) for p in parts] + [right]
                w = jnp.concatenate(
                    [
                        jnp.where(spot == 0, right_turned[t], right_turned[t + 1])
                        for t in range(tiles)
                    ],
                    axis=1,
                )
                e = jnp.concatenate(
                    [
                        jnp.where(spot == 127, left_turned[t + 1], left_turned[t])
                        for t in range(tiles)
                    ],
                    axis=1,
                )
                y = (
                    x
                    + east_w * (e - x)
                    + west_w * (w - x)
                    + north_w * (n - x)
                    + south_w * (s - x)
                )
                results[r, field, span] = y

    def combine(i):
        half_copy(i).wait_recv()
        total = partial[i, own] + half_in[i]
        partial[i, own] = total
        largest = jnp.maximum(jnp.max(jnp.abs(total), axis=1, keepdims=True), 1e-30)
        power = jnp.ceil(jnp.log2(largest))
        code = jnp.round(total * (jnp.exp2(-power) * 32767.0))
        code = jnp.clip(code, -32767.0, 32767.0)
        place = lax.broadcasted_iota(jnp.int32, (half, 2 * KC), 1)
        code = jnp.where(place == KC, power, code)
        coded[i] = code.astype(jnp.int32).astype(jnp.int16)

    wave = lax.rem(lax.broadcasted_iota(jnp.int32, (8, 2 * KC), 1), KC)
    weight = jnp.where(wave == 0, 1.0 / circle_size, 2.0 / circle_size).astype(jnp.float32)

    def finish(i):
        code_copy(i).wait_recv()
        code = coded_in[i].astype(jnp.int32).astype(jnp.float32)
        unit = jnp.exp2(code[:, KC : KC + 1]) * (1.0 / 32767.0)
        place = lax.broadcasted_iota(jnp.int32, (half, 2 * KC), 1)
        code = jnp.where(place == KC, 0.0, code)
        total = partial[i, own] + code * unit
        limit = cutoff[lat * rows + row_at(i)]
        scale = jnp.where(wave <= limit, weight, 0.0)
        scaled = total.reshape(half // 8, 8, 2 * KC) * scale[None]
        spectra[i, own] = scaled.reshape(half, 2 * KC).astype(jnp.bfloat16)
        join_copy(i).start()

    def merge(i):
        join_copy(i).wait_recv()
        r = row_at(i)
        smooth = jnp.dot(spectra[i], turned[...], preferred_element_type=jnp.float32)
        smooth = smooth.astype(jnp.bfloat16).astype(jnp.float32)
        smooth = smooth.reshape(fields, levels, columns)
        kept = jnp.full((8, columns), mask[lat * rows + r], jnp.int32) != 0
        for field in range(fields):
            for group in range(groups):
                span = pl.ds(group * 8, 8)
                results[r, field, span] = jnp.where(
                    kept, smooth[field, group * 8 : group * 8 + 8], results[r, field, span]
                )

    def take_halo(side):
        for field in range(fields):
            edge_copy(0, field, side, (lat, across)).wait_recv()
        xs[side * (rows + 1)] = halos[side].astype(jnp.float32)

    def send_code(i):
        @pl.when(i < RELAYED)
        def _():
            lend_copy(i).start()

        @pl.when(i >= RELAYED)
        def _():
            code_copy(i).start()

    def advance(i, carry):
        r = row_at(i)

        @pl.when(i == rows - 2)
        def _():
            @pl.when(middle)
            def _():
                for p in range(RELAYED):
                    lend_copy(p).wait_recv()
                    pass_copy(p).start()

        @pl.when((i >= rows - 2) & (r == 0))
        def _():
            take_halo(0)

        @pl.when((i >= rows - 2) & (r == rows - 1))
        def _():
            take_halo(1)

        column_copy(0, r, (lat, after)).wait_recv()
        column_copy(1, r, (lat, before)).wait_recv()
        weight_copy(r).wait()
        step(r)

        @pl.when(polar)
        def _():
            rounded[...] = results[r].reshape(lines, columns).astype(jnp.bfloat16)
            partial[i] = jnp.dot(rounded[...], waves[...], preferred_element_type=jnp.float32)
            half_copy(i).start()

            @pl.when(i >= 1)
            def _():
                combine(i - 1)
                send_code(i - 1)

        return carry

    lax.fori_loop(0, rows, advance, 0)

    @pl.when(polar)
    def _():
        combine(rows - 1)
        send_code(rows - 1)

        def position(t):
            return t // 2 + (rows // 2) * lax.rem(t, 2)

        def endings(t, carry):
            finish(position(t))

            @pl.when(t >= 1)
            def _():
                merge(position(t - 1))

            return carry

        lax.fori_loop(0, rows, endings, 0)
        merge(position(rows - 1))

        def drain(i, carry):
            half_copy(i).wait_send()
            code_copy(i).wait_send()
            join_copy(i).wait_send()
            return carry

        lax.fori_loop(0, rows, drain, 0)

    @pl.when(middle)
    def _():
        for p in range(RELAYED):
            pass_copy(p).wait_send()

    for field in range(fields):
        for k in range(2):
            edge_copy(k, field, 0, (lat, across)).wait_send()
    for r in range(rows):
        for k in range(2):
            column_copy(k, r, (lat, after)).wait_send()


def place_kernel(stepped, out, sem):
    copies = [
        pltpu.make_async_copy(stepped.at[r], out.at[:, :, r], sem.at[r])
        for r in range(stepped.shape[0])
    ]
    for copy in copies:
        copy.start()
    for copy in copies:
        copy.wait()


def with_caps(state_fields, stencil_weights, filter_mask, cutoff_wave):
    fields, levels, rows, columns = state_fields.shape
    lon_count = lax.axis_size("lon")
    lines = fields * levels
    half = lines // 2
    table = roots_table(columns, columns * lon_count)
    dma = pltpu.SemaphoreType.DMA
    in_hbm = pl.BlockSpec(memory_space=pl.ANY)
    in_vmem = pl.BlockSpec(memory_space=pltpu.VMEM)
    f32, bf16, i16 = jnp.float32, jnp.bfloat16, jnp.int16
    stepped = pl.pallas_call(
        caps_kernel,
        in_specs=[in_hbm] * 6,
        out_specs=in_vmem,
        out_shape=jax.ShapeDtypeStruct((rows, fields, levels, columns), f32),
        scratch_shapes=[
            pltpu.VMEM((rows + 2, fields, levels, columns), f32),
            pltpu.VMEM((rows, 4, levels, columns), f32),
            pltpu.VMEM((columns, 2 * KC), bf16),
            pltpu.VMEM((2 * KC, columns), bf16),
            pltpu.SMEM(filter_mask.shape, jnp.int32),
            pltpu.SMEM(cutoff_wave.shape, jnp.int32),
            pltpu.VMEM((lines, columns), bf16),
            pltpu.VMEM((2, fields, levels, columns), bf16),
            pltpu.VMEM((2, fields, levels, columns), bf16),
            pltpu.VMEM((2, rows, 8, 128), f32),
            pltpu.VMEM((2, rows, 8, 128), f32),
            pltpu.VMEM((rows, lines, 2 * KC), f32),
            pltpu.VMEM((rows, half, 2 * KC), f32),
            pltpu.VMEM((rows, half, 2 * KC), i16),
            pltpu.VMEM((rows, half, 2 * KC), i16),
            pltpu.VMEM((RELAYED, half, 2 * KC), i16),
            pltpu.VMEM((rows, lines, 2 * KC), bf16),
            dma((rows,)),
            dma((rows,)),
            dma((4,)),
            dma((2, fields)),
            dma((2, fields)),
            dma((2, rows)),
            dma((2, rows)),
            dma((rows,)),
            dma((rows,)),
            dma((rows,)),
            dma((rows,)),
            dma((RELAYED,)),
            dma((RELAYED,)),
            dma((rows,)),
            dma((rows,)),
        ],
        compiler_params=pltpu.CompilerParams(
            collective_id=1, has_side_effects=True, vmem_limit_bytes=40_000_000
        ),
        name="caps",
    )(
        *(
            pltpu.with_memory_space_constraint(array, pltpu.HBM)
            for array in (
                state_fields,
                stencil_weights,
                filter_mask,
                cutoff_wave,
                jnp.asarray(table),
                jnp.asarray(np.ascontiguousarray(table.T)),
            )
        )
    )
    return pl.pallas_call(
        place_kernel,
        in_specs=[in_vmem],
        out_specs=in_hbm,
        out_shape=jax.ShapeDtypeStruct(state_fields.shape, f32),
        scratch_shapes=[dma((rows,))],
        compiler_params=pltpu.CompilerParams(vmem_limit_bytes=1 << 20),
        name="place",
    )(stepped)


def cap_rows(lat_rows):
    return {64: 8, 256: 40}.get(lat_rows, lat_rows)


def solution(mesh):
    def body(state_fields, stencil_weights, filter_mask, cutoff_wave):
        fields, levels, rows, columns = state_fields.shape
        one_block = cap_rows(filter_mask.shape[0]) <= rows
        suits = rows == 8 and columns % 128 == 0 and fields * levels % 32 == 0 and levels % 16 == 0
        if one_block and suits and mesh.shape["lon"] == 4 and mesh.shape["lat"] >= 6:
            return with_caps(state_fields, stencil_weights, filter_mask, cutoff_wave)
        return on_device(state_fields, stencil_weights, filter_mask, cutoff_wave)

    return jax.shard_map(
        body,
        mesh=mesh,
        in_specs=(P(None, None, "lat", "lon"), P(None, None, "lat", "lon"), P(), P()),
        out_specs=P(None, None, "lat", "lon"),
        check_vma=False,
    )
```

profile of v0, /device:TPU:0, one launch (start us, length us, event | category | flops | bytes accessed | tf_op | source)
XLA Modules:
  0.0 28.9 jit_solution(10213147480790723944)
XLA Ops:
  0.0 26.5 %caps.1.stepped = f32[8,5,32,1024]{3,2,1,0:T(8,128)S(1)} custom-call(f32[5,32,8,1024]{3,2,1,0:T(8,128)} %state.1, f32[4,32,8,1024]{3,2,1,0:T(8,128)} %weights.1, s32[64]{0:T(128)} %mask_in.1, s32[64]{0:T(128)} %cutoff_in.1, bf16[1024,512]{1,0:T(8,128)(2,1)} %constant.4.clone.waves_in, bf16[512,1024]{1,0:T(8,128)(2,1)} %constant.5.clone.turned_in), custom_call_target="tpu_custom_call" | custom-call | tf_op jit(solution)/shard_map/caps/pallas_call | solution.py:933
  26.5 2.4 %place.1 = f32[5,32,8,1024]{3,2,1,0:T(8,128)} custom-call(f32[8,5,32,1024]{3,2,1,0:T(8,128)S(1)} %caps.1.stepped), custom_call_target="tpu_custom_call" | custom-call | tf_op jit(solution)/shard_map/place/pallas_call | solution.py:989
where the time goes:
time: 29.1 us; the launch traced here: 28.9 us
  Pallas kernels  28.9 us (99%)
    pallas_call x1, Pallas kernels, with_caps(): pl.pallas_call(caps_kernel, in_specs=[in_hbm] * 6, out_specs=in_vmem, out...  26.5 us
    pallas_call x1, Pallas kernels, with_caps(): pl.pallas_call(place_kernel, in_specs=[in_vmem], out_specs=in_hbm, out_sh...  2.42 us

commit v1 on v0

--- a/solution.py
+++ b/solution.py
@@ -454,11 +454,10 @@
     phase = lax.rem(lax.broadcasted_iota(jnp.int32, shape, axis) * turns, 4)
     a = jnp.where(phase == 0, 1.0, jnp.where(phase == 2, -1.0, 0.0))
     b = jnp.where(phase == 1, 1.0, jnp.where(phase == 3, -1.0, 0.0))
-    return a.astype(jnp.float32), b.astype(jnp.float32)
+    return a.astype(jnp.bfloat16), b.astype(jnp.bfloat16)
 
 
 RELAYED = 4
-FINISH = (0, 4, 1, 5, 2, 6, 3, 7)
 
 
 def caps_kernel(
@@ -475,7 +474,8 @@
     turned,
     mask,
     cutoff,
-    rounded,
+    even_lines,
+    odd_lines,
     edges,
     halos,
     columns_out,
@@ -559,7 +559,7 @@
         return remote(
             edges.at[k, field],
             halos.at[side, field],
-            edge_send.at[k, field],
+            edge_send.at[k],
             edge_recv.at[side, field],
             device,
         )
@@ -568,7 +568,7 @@
         return remote(
             columns_out.at[k, r],
             columns_in.at[k, r],
-            column_send.at[k, r],
+            column_send.at[k],
             column_recv.at[k, r],
             device,
         )
@@ -597,18 +597,24 @@
         view = spectra.at[i, own]
         return remote(view, view, join_send.at[i], join_recv.at[i], (lat, partner))
 
-    order = (0, rows - 1, *range(1, rows - 1))
-    for r in order:
+    for r in (0, rows - 1, *range(1, rows - 1)):
         state_copy(r).start()
     for copy in bound_copies():
         copy.start()
-    for r in (*range(1, rows - 1), 0, rows - 1):
+    for r in range(1, rows - 1):
         weight_copy(r).start()
+        if r == 2:
+
+            @pl.when(polar)
+            def _():
+                table_copies()[0].start()
+
+    weight_copy(0).start()
+    weight_copy(rows - 1).start()
 
     @pl.when(polar)
     def _():
-        for copy in table_copies():
-            copy.start()
+        table_copies()[1].start()
 
     barrier = pltpu.get_barrier_semaphore()
 
@@ -703,75 +709,91 @@
     for copy in bound_copies():
         copy.wait()
 
-    @pl.when(polar)
-    def _():
-        for copy in table_copies():
-            copy.wait()
+    def turn_waves():
+        table_copies()[0].wait()
         a, b = quarter_turns((16, KC), 1, lon)
 
-        def turn_waves(t, carry):
-            span = pl.ds(pl.multiple_of(t * 16, 16), 16)
-            c = waves[span, :KC].astype(jnp.float32)
-            s = waves[span, KC:].astype(jnp.float32)
-            waves[span, :KC] = (a * c - b * s).astype(jnp.bfloat16)
-            waves[span, KC:] = (a * s + b * c).astype(jnp.bfloat16)
+        def turn(t, carry):
+            for u in range(4):
+                span = pl.ds(pl.multiple_of(t * 64 + u * 16, 16), 16)
+                c, s = waves[span, :KC], waves[span, KC:]
+                waves[span, :KC] = a * c - b * s
+                waves[span, KC:] = a * s + b * c
             return carry
 
-        lax.fori_loop(0, columns // 16, turn_waves, 0)
-        u, v = quarter_turns((16, 128), 0, lon)
-
-        def turn_back(t, carry):
+        lax.fori_loop(0, columns // 64, turn, 0)
+
+    def turn_back():
+        table_copies()[1].wait()
+        a, b = quarter_turns((16, 128), 0, lon)
+
+        def turn(t, carry):
             low = pl.ds(pl.multiple_of(t * 16, 16), 16)
             high = pl.ds(pl.multiple_of(KC + t * 16, 16), 16)
             for tile in range(columns // 128):
                 lanes = pl.ds(tile * 128, 128)
-                c = turned[low, lanes].astype(jnp.float32)
-                s = turned[high, lanes].astype(jnp.float32)
-                turned[low, lanes] = (u * c - v * s).astype(jnp.bfloat16)
-                turned[high, lanes] = (u * s + v * c).astype(jnp.bfloat16)
+                c, s = turned[low, lanes], turned[high, lanes]
+                turned[low, lanes] = a * c - b * s
+                turned[high, lanes] = a * s + b * c
             return carry
 
-        lax.fori_loop(0, KC // 16, turn_back, 0)
+        lax.fori_loop(0, KC // 16, turn, 0)
 
     tiles = columns // 128
+
+    def shares(r, group):
+        span = pl.ds(group * 8, 8)
+        return [ws[r, q, span] for q in range(4)]
+
+    def advanced(r, field, group, east_w, west_w, north_w, south_w):
+        at = group * fields + field
+        span = pl.ds(group * 8, 8)
+        x = xs[r + 1, field, span]
+        n = xs[r, field, span]
+        s = xs[r + 2, field, span]
+        parts = [x[:, t * 128 : t * 128 + 128] for t in range(tiles)]
+        left = columns_in[0, r]
+        left = pltpu.roll(left, 128 - at, 1) if at else left
+        right = pltpu.roll(columns_in[1, r], 127 - at, 1)
+        to_right = [left] + [pltpu.roll(p, 1, 1) for p in parts]
+        to_left = [pltpu.roll(p, 127, 1) for p in parts] + [right]
+        w = [jnp.where(spot == 0, to_right[t], to_right[t + 1]) for t in range(tiles)]
+        e = [jnp.where(spot == 127, to_left[t + 1], to_left[t]) for t in range(tiles)]
+        y = (
+            x
+            + east_w * (jnp.concatenate(e, axis=1) - x)
+            + west_w * (jnp.concatenate(w, axis=1) - x)
+            + north_w * (n - x)
+            + south_w * (s - x)
+        )
+        results[r, field, span] = y
+        return y
+
+    def ready(r):
+        column_copy(0, r, (lat, after)).wait_recv()
+        column_copy(1, r, (lat, before)).wait_recv()
+        weight_copy(r).wait()
 
     def step(r):
         for group in range(groups):
-            span = pl.ds(group * 8, 8)
-            east_w, west_w, north_w, south_w = (ws[r, q, span] for q in range(4))
+            weight = shares(r, group)
             for field in range(fields):
-                at = group * fields + field
-                x = xs[r + 1, field, span]
-                n = xs[r, field, span]
-                s = xs[r + 2, field, span]
-                parts = [x[:, t * 128 : t * 128 + 128] for t in range(tiles)]
-                left = columns_in[0, r]
-                left = pltpu.roll(left, 128 - at, 1) if at else left
-                right = pltpu.roll(columns_in[1, r], 127 - at, 1)
-                right_turned = [left] + [pltpu.roll(p, 1, 1) for p in parts]
-                left_turned = [pltpu.roll(p, 127, 1) for p in parts] + [right]
-                w = jnp.concatenate(
-                    [
-                        jnp.where(spot == 0, right_turned[t], right_turned[t + 1])
-                        for t in range(tiles)
-                    ],
-                    axis=1,
+                advanced(r, field, group, *weight)
+
+    def step_into(r, target):
+        for group in range(0, groups, 2):
+            weight, next_weight = shares(r, group), shares(r, group + 1)
+            for field in range(fields):
+                pair = (
+                    advanced(r, field, group, *weight),
+                    advanced(r, field, group + 1, *next_weight),
                 )
-                e = jnp.concatenate(
-                    [
-                        jnp.where(spot == 127, left_turned[t + 1], left_turned[t])
-                        for t in range(tiles)
-                    ],
-                    axis=1,
-                )
-                y = (
-                    x
-                    + east_w * (e - x)
-                    + west_w * (w - x)
-                    + north_w * (n - x)
-                    + south_w * (s - x)
-                )
-                results[r, field, span] = y
+                target[pl.ds(field * levels + group * 8, 16)] = jnp.concatenate(
+                    pair, axis=0
+                ).astype(jnp.bfloat16)
+
+    def transform(source, i):
+        partial[i] = jnp.dot(source[...], waves[...], preferred_element_type=jnp.float32)
 
     def combine(i):
         half_copy(i).wait_recv()
@@ -815,11 +837,6 @@
                     kept, smooth[field, group * 8 : group * 8 + 8], results[r, field, span]
                 )
 
-    def take_halo(side):
-        for field in range(fields):
-            edge_copy(0, field, side, (lat, across)).wait_recv()
-        xs[side * (rows + 1)] = halos[side].astype(jnp.float32)
-
     def send_code(i):
         @pl.when(i < RELAYED)
         def _():
@@ -829,63 +846,98 @@
         def _():
             code_copy(i).start()
 
-    def advance(i, carry):
-        r = row_at(i)
-
-        @pl.when(i == rows - 2)
-        def _():
-            @pl.when(middle)
+    def combine_and_send(i):
+        combine(i)
+        send_code(i)
+
+    pairs = (rows - 2) // 2
+
+    @pl.when(polar)
+    def _():
+        turn_waves()
+        odd_lines[...] = jnp.zeros_like(odd_lines)
+
+        def two_rows(j, carry):
+            i = 2 * j
+            ready(i + 1)
+            transform(odd_lines, jnp.where(j == 0, rows, i - 1))
+            step_into(i + 1, even_lines)
+
+            @pl.when(j >= 1)
             def _():
-                for p in range(RELAYED):
-                    lend_copy(p).wait_recv()
-                    pass_copy(p).start()
-
-        @pl.when((i >= rows - 2) & (r == 0))
-        def _():
-            take_halo(0)
-
-        @pl.when((i >= rows - 2) & (r == rows - 1))
-        def _():
-            take_halo(1)
-
-        column_copy(0, r, (lat, after)).wait_recv()
-        column_copy(1, r, (lat, before)).wait_recv()
-        weight_copy(r).wait()
-        step(r)
-
-        @pl.when(polar)
-        def _():
-            rounded[...] = results[r].reshape(lines, columns).astype(jnp.bfloat16)
-            partial[i] = jnp.dot(rounded[...], waves[...], preferred_element_type=jnp.float32)
+                half_copy(i - 1).start()
+
+            @pl.when(j >= 2)
+            def _():
+                combine_and_send(i - 3)
+
+            ready(i + 2)
+            transform(even_lines, i)
+            step_into(i + 2, odd_lines)
             half_copy(i).start()
 
-            @pl.when(i >= 1)
+            @pl.when(j >= 1)
             def _():
-                combine(i - 1)
-                send_code(i - 1)
-
-        return carry
-
-    lax.fori_loop(0, rows, advance, 0)
+                combine_and_send(i - 2)
+
+            return carry
+
+        lax.fori_loop(0, pairs, two_rows, 0)
+        transform(odd_lines, rows - 3)
+        half_copy(rows - 3).start()
+        combine_and_send(rows - 5)
+        turn_back()
+        combine_and_send(rows - 4)
+        combine_and_send(rows - 3)
+
+    @pl.when(jnp.logical_not(polar))
+    def _():
+        def one_row(r, carry):
+            ready(r)
+            step(r)
+            return carry
+
+        lax.fori_loop(1, rows - 1, one_row, 0)
+
+    @pl.when(middle)
+    def _():
+        for p in range(RELAYED):
+            lend_copy(p).wait_recv()
+            pass_copy(p).start()
+
+    ready(0)
+    ready(rows - 1)
+    for field in range(fields):
+        for side, r in ((1, rows - 1), (0, 0)):
+            edge_copy(0, field, side, (lat, across)).wait_recv()
+            xs[side * (rows + 1), field] = halos[side, field].astype(jnp.float32)
+            for group in range(groups):
+                advanced(r, field, group, *shares(r, group))
 
     @pl.when(polar)
     def _():
-        combine(rows - 1)
-        send_code(rows - 1)
+        for i, lines_of in ((rows - 2, even_lines), (rows - 1, odd_lines)):
+            r = row_at(i)
+            lines_of[...] = results[r].reshape(lines, columns).astype(jnp.bfloat16)
+            transform(lines_of, i)
+            half_copy(i).start()
+        combine_and_send(rows - 2)
+        combine_and_send(rows - 1)
 
         def position(t):
-            return t // 2 + (rows // 2) * lax.rem(t, 2)
+            return t // 2 + (rows // 2) * (1 - lax.rem(t, 2))
 
         def endings(t, carry):
             finish(position(t))
 
-            @pl.when(t >= 1)
+            @pl.when(t >= 2)
             def _():
-                merge(position(t - 1))
+                merge(position(t - 2))
 
             return carry
 
         lax.fori_loop(0, rows, endings, 0)
+        merge(position(rows - 2))
         merge(position(rows - 1))
 
         def drain(i, carry):
@@ -901,12 +953,17 @@
         for p in range(RELAYED):
             pass_copy(p).wait_send()
 
-    for field in range(fields):
-        for k in range(2):
-            edge_copy(k, field, 0, (lat, across)).wait_send()
-    for r in range(rows):
-        for k in range(2):
-            column_copy(k, r, (lat, after)).wait_send()
+    for k in range(2):
+        remote(
+            edges.at[k], halos.at[k], edge_send.at[k], edge_recv.at[k, 0], (lat, across)
+        ).wait_send()
+        remote(
+            columns_out.at[k],
+            columns_in.at[k],
+            column_send.at[k],
+            column_recv.at[k, 0],
+            (lat, after),
+        ).wait_send()
 
 
 def place_kernel(stepped, out, sem):
@@ -943,11 +1000,12 @@
             pltpu.SMEM(filter_mask.shape, jnp.int32),
             pltpu.SMEM(cutoff_wave.shape, jnp.int32),
             pltpu.VMEM((lines, columns), bf16),
+            pltpu.VMEM((lines, columns), bf16),
             pltpu.VMEM((2, fields, levels, columns), bf16),
             pltpu.VMEM((2, fields, levels, columns), bf16),
             pltpu.VMEM((2, rows, 8, 128), f32),
             pltpu.VMEM((2, rows, 8, 128), f32),
-            pltpu.VMEM((rows, lines, 2 * KC), f32),
+            pltpu.VMEM((rows + 1, lines, 2 * KC), f32),
             pltpu.VMEM((rows, half, 2 * KC), f32),
             pltpu.VMEM((rows, half, 2 * KC), i16),
             pltpu.VMEM((rows, half, 2 * KC), i16),
@@ -956,9 +1014,9 @@
             dma((rows,)),
             dma((rows,)),
             dma((4,)),
+            dma((2,)),
             dma((2, fields)),
-            dma((2, fields)),
-            dma((2, rows)),
+            dma((2,)),
             dma((2, rows)),
             dma((rows,)),
             dma((rows,)),

time: 29.1 us -> 29.1 us (level)
  no operation moved by 1% of the time
where the time goes in v1:
time: 29.1 us; the launch traced here: 28.8 us
  Pallas kernels  28.8 us (99%)
    pallas_call x1, Pallas kernels, with_caps(): pl.pallas_call(caps_kernel, in_specs=[in_hbm] * 6, out_specs=in_vmem, out...  26.4 us
    pallas_call x1, Pallas kernels, with_caps(): pl.pallas_call(place_kernel, in_specs=[in_vmem], out_specs=in_hbm, out_sh...  2.42 us

profile of v1, /device:TPU:0, one launch (start us, length us, event | category | flops | bytes accessed | tf_op | source)
XLA Modules:
  0.0 28.8 jit_solution(11691905649498098201)
XLA Ops:
  0.0 26.4 %caps.1.stepped = f32[8,5,32,1024]{3,2,1,0:T(8,128)S(1)} custom-call(f32[5,32,8,1024]{3,2,1,0:T(8,128)} %state.1, f32[4,32,8,1024]{3,2,1,0:T(8,128)} %weights.1, s32[64]{0:T(128)} %mask_in.1, s32[64]{0:T(128)} %cutoff_in.1, bf16[1024,512]{1,0:T(8,128)(2,1)} %constant.4.clone.waves_in, bf16[512,1024]{1,0:T(8,128)(2,1)} %constant.5.clone.turned_in), custom_call_target="tpu_custom_call" | custom-call | tf_op jit(solution)/shard_map/caps/pallas_call | solution.py:990
  26.4 2.4 %place.1 = f32[5,32,8,1024]{3,2,1,0:T(8,128)} custom-call(f32[8,5,32,1024]{3,2,1,0:T(8,128)S(1)} %caps.1.stepped), custom_call_target="tpu_custom_call" | custom-call | tf_op jit(solution)/shard_map/place/pallas_call | solution.py:1047

commit v2 on v1

--- a/solution.py
+++ b/solution.py
@@ -457,7 +457,7 @@
     return a.astype(jnp.bfloat16), b.astype(jnp.bfloat16)
 
 
-RELAYED = 4
+RELAYED = 3
 
 
 def caps_kernel(
@@ -497,6 +497,8 @@
     half_recv,
     code_send,
     code_recv,
+    lend_send,
+    lend_recv,
     pass_send,
     pass_recv,
     join_send,
@@ -545,7 +547,7 @@
 
     def table_copies():
         return (
-            pltpu.make_async_copy(waves_in, waves, table_sem.at[0]),
+            pltpu.make_async_copy(waves_in.at[core], waves, table_sem.at[0]),
             pltpu.make_async_copy(turned_in, turned, table_sem.at[1]),
         )
 
@@ -583,64 +585,72 @@
             coded.at[i], coded_in.at[i], code_send.at[i], code_recv.at[i], (lat, across)
         )
 
-    def lend_copy(i):
+    first_piece = (half // 2 + 15) // 16 * 16
+    pieces = (pl.ds(0, first_piece), pl.ds(first_piece, half - first_piece))
+
+    def lend_copy(i, k):
         return remote(
-            coded.at[i], passing.at[i], code_send.at[i], pass_recv.at[i], (helper, across)
-        )
-
-    def pass_copy(i):
+            coded.at[i, pieces[k]],
+            passing.at[i, pieces[k]],
+            lend_send.at[i, k],
+            pass_recv.at[i, k],
+            (helper, across),
+        )
+
+    def pass_copy(i, k):
         return remote(
-            passing.at[i], coded_in.at[i], pass_send.at[i], code_recv.at[i], (served, lon)
+            passing.at[i, pieces[k]],
+            coded_in.at[i, pieces[k]],
+            pass_send.at[i, k],
+            lend_recv.at[i, k],
+            (served, lon),
         )
 
     def join_copy(i):
         view = spectra.at[i, own]
         return remote(view, view, join_send.at[i], join_recv.at[i], (lat, partner))
 
+    barrier = pltpu.get_barrier_semaphore()
+
+    def greet(a, b):
+        pl.semaphore_signal(barrier, inc=1, device_id=(a, b), device_id_type=MESH)
+
+    for b in (after, before, across):
+        greet(lat, b)
+
+    @pl.when(lat > 0)
+    def _():
+        greet(lat - 1, lon)
+
+    @pl.when(lat < lat_count - 1)
+    def _():
+        greet(lat + 1, lon)
+
+    @pl.when(polar)
+    def _():
+        greet(helper, lon)
+        greet(helper, across)
+
+    @pl.when(middle)
+    def _():
+        greet(served, lon)
+        greet(served, across)
+
     for r in (0, rows - 1, *range(1, rows - 1)):
         state_copy(r).start()
+
+    @pl.when(polar)
+    def _():
+        table_copies()[0].start()
+
     for copy in bound_copies():
         copy.start()
-    for r in range(1, rows - 1):
+    for r in (*range(1, rows - 1), 0, rows - 1):
         weight_copy(r).start()
-        if r == 2:
-
-            @pl.when(polar)
-            def _():
-                table_copies()[0].start()
-
-    weight_copy(0).start()
-    weight_copy(rows - 1).start()
 
     @pl.when(polar)
     def _():
         table_copies()[1].start()
-
-    barrier = pltpu.get_barrier_semaphore()
-
-    def greet(a, b):
-        pl.semaphore_signal(barrier, inc=1, device_id=(a, b), device_id_type=MESH)
-
-    for b in (after, before, across):
-        greet(lat, b)
-
-    @pl.when(lat > 0)
-    def _():
-        greet(lat - 1, lon)
-
-    @pl.when(lat < lat_count - 1)
-    def _():
-        greet(lat + 1, lon)
-
-    @pl.when(polar)
-    def _():
-        greet(helper, lon)
-        greet(helper, across)
-
-    @pl.when(middle)
-    def _():
-        greet(served, lon)
-        greet(served, across)
 
     for r in (0, rows - 1):
         state_copy(r).wait()
@@ -663,15 +673,37 @@
     def _():
         pl.semaphore_wait(barrier, 3 + 2)
 
-    for field in range(fields):
-
+    def send_up(field):
         @pl.when(lat > 0)
         def _():
             edge_copy(0, field, 1, (lat - 1, lon)).start()
 
+    def send_down(field):
         @pl.when(lat < lat_count - 1)
         def _():
             edge_copy(1, field, 0, (lat + 1, lon)).start()
+
+    beside_first, beside_last = lat == 1, lat == lat_count - 2
+
+    @pl.when(beside_first)
+    def _():
+        for field in range(fields):
+            send_up(field)
+        for field in range(fields):
+            send_down(field)
+
+    @pl.when(beside_last)
+    def _():
+        for field in range(fields):
+            send_down(field)
+        for field in range(fields):
+            send_up(field)
+
+    @pl.when(jnp.logical_not(beside_first | beside_last))
+    def _():
+        for field in range(fields):
+            send_up(field)
+            send_down(field)
 
     spot = lax.broadcasted_iota(jnp.int32, (8, 128), 1)
 
@@ -692,40 +724,30 @@
         column_copy(0, r, (lat, after)).start()
         column_copy(1, r, (lat, before)).start()
 
-    for j, r in enumerate((*range(1, rows - 1), rows - 1, 0)):
+    def send_rim(field):
+        @pl.when(first)
+        def _():
+            edge_copy(0, field, 0, (lat, across)).start()
+
+        @pl.when(last)
+        def _():
+            edge_copy(1, field, 1, (lat, across)).start()
+
+    for r in (*range(1, rows - 1), rows - 1, 0):
         if 0 < r < rows - 1:
             state_copy(r).wait()
         send_columns(r)
-        if 1 <= j <= fields:
-
-            @pl.when(first)
-            def _():
-                edge_copy(0, j - 1, 0, (lat, across)).start()
-
-            @pl.when(last)
-            def _():
-                edge_copy(1, j - 1, 1, (lat, across)).start()
+        if r == 3:
+            send_rim(0)
+    for field in range(1, fields):
+        send_rim(field)
 
     for copy in bound_copies():
         copy.wait()
 
-    def turn_waves():
-        table_copies()[0].wait()
-        a, b = quarter_turns((16, KC), 1, lon)
-
-        def turn(t, carry):
-            for u in range(4):
-                span = pl.ds(pl.multiple_of(t * 64 + u * 16, 16), 16)
-                c, s = waves[span, :KC], waves[span, KC:]
-                waves[span, :KC] = a * c - b * s
-                waves[span, KC:] = a * s + b * c
-            return carry
-
-        lax.fori_loop(0, columns // 64, turn, 0)
-
     def turn_back():
         table_copies()[1].wait()
-        a, b = quarter_turns((16, 128), 0, lon)
+        a, b = quarter_turns((16, 128), 0, core)
 
         def turn(t, carry):
             low = pl.ds(pl.multiple_of(t * 16, 16), 16)
@@ -811,11 +833,20 @@
     weight = jnp.where(wave == 0, 1.0 / circle_size, 2.0 / circle_size).astype(jnp.float32)
 
     def finish(i):
-        code_copy(i).wait_recv()
+        @pl.when(i < RELAYED)
+        def _():
+            for k in range(2):
+                pass_copy(i, k).wait_recv()
+
+        @pl.when(i >= RELAYED)
+        def _():
+            code_copy(i).wait_recv()
+
         code = coded_in[i].astype(jnp.int32).astype(jnp.float32)
         unit = jnp.exp2(code[:, KC : KC + 1]) * (1.0 / 32767.0)
         place = lax.broadcasted_iota(jnp.int32, (half, 2 * KC), 1)
-        code = jnp.where(place == KC, 0.0, code)
+        turned_by = jnp.where(lax.rem(place, 2) == 0, 1.0, -1.0)
+        code = code * jnp.where(place == KC, 0.0, turned_by)
         total = partial[i, own] + code * unit
         limit = cutoff[lat * rows + row_at(i)]
         scale = jnp.where(wave <= limit, weight, 0.0)
@@ -840,7 +871,8 @@
     def send_code(i):
         @pl.when(i < RELAYED)
         def _():
-            lend_copy(i).start()
+            for k in range(2):
+                lend_copy(i, k).start()
 
         @pl.when(i >= RELAYED)
         def _():
@@ -854,7 +886,7 @@
 
     @pl.when(polar)
     def _():
-        turn_waves()
+        table_copies()[0].wait()
         odd_lines[...] = jnp.zeros_like(odd_lines)
 
         def two_rows(j, carry):
@@ -869,26 +901,27 @@
 
             @pl.when(j >= 2)
             def _():
-                combine_and_send(i - 3)
+                combine_and_send(i - 4)
 
             ready(i + 2)
             transform(even_lines, i)
             step_into(i + 2, odd_lines)
             half_copy(i).start()
 
-            @pl.when(j >= 1)
+            @pl.when(j >= 2)
             def _():
-                combine_and_send(i - 2)
+                combine_and_send(i - 3)
 
             return carry
 
         lax.fori_loop(0, pairs, two_rows, 0)
         transform(odd_lines, rows - 3)
         half_copy(rows - 3).start()
+        combine_and_send(rows - 6)
         combine_and_send(rows - 5)
-        turn_back()
         combine_and_send(rows - 4)
         combine_and_send(rows - 3)
+        turn_back()
 
     @pl.when(jnp.logical_not(polar))
     def _():
@@ -902,8 +935,9 @@
     @pl.when(middle)
     def _():
         for p in range(RELAYED):
-            lend_copy(p).wait_recv()
-            pass_copy(p).start()
+            for k in range(2):
+                lend_copy(p, k).wait_recv()
+                pass_copy(p, k).start()
 
     ready(0)
     ready(rows - 1)
@@ -921,29 +955,38 @@
             lines_of[...] = results[r].reshape(lines, columns).astype(jnp.bfloat16)
             transform(lines_of, i)
             half_copy(i).start()
+        def position(t):
+            return jnp.where(t < 2 * RELAYED, t // 2 + RELAYED * (1 - lax.rem(t, 2)), t)
+
+        finish(position(0))
+        finish(position(1))
         combine_and_send(rows - 2)
         combine_and_send(rows - 1)
 
-        def position(t):
-            return t // 2 + (rows // 2) * (1 - lax.rem(t, 2))
-
         def endings(t, carry):
+            merge(position(t - 2))
             finish(position(t))
-
-            @pl.when(t >= 2)
-            def _():
-                merge(position(t - 2))
-
             return carry
 
-        lax.fori_loop(0, rows, endings, 0)
+        lax.fori_loop(2, rows - 1, endings, 0)
+        merge(position(rows - 3))
         merge(position(rows - 2))
-        merge(position(rows - 1))
+        finish(rows - 1)
+        merge(rows - 1)
 
         def drain(i, carry):
             half_copy(i).wait_send()
-            code_copy(i).wait_send()
             join_copy(i).wait_send()
+
+            @pl.when(i < RELAYED)
+            def _():
+                for k in range(2):
+                    lend_copy(i, k).wait_send()
+
+            @pl.when(i >= RELAYED)
+            def _():
+                code_copy(i).wait_send()
+
             return carry
 
         lax.fori_loop(0, rows, drain, 0)
@@ -951,7 +994,8 @@
     @pl.when(middle)
     def _():
         for p in range(RELAYED):
-            pass_copy(p).wait_send()
+            for k in range(2):
+                pass_copy(p, k).wait_send()
 
     for k in range(2):
         remote(
@@ -982,7 +1026,8 @@
     lon_count = lax.axis_size("lon")
     lines = fields * levels
     half = lines // 2
-    table = roots_table(columns, columns * lon_count)
+    whole_table = roots_table(2 * columns, columns * lon_count)
+    table = whole_table[:columns]
     dma = pltpu.SemaphoreType.DMA
     in_hbm = pl.BlockSpec(memory_space=pl.ANY)
     in_vmem = pl.BlockSpec(memory_space=pltpu.VMEM)
@@ -1022,8 +1067,10 @@
             dma((rows,)),
             dma((rows,)),
             dma((rows,)),
-            dma((RELAYED,)),
-            dma((RELAYED,)),
+            dma((RELAYED, 2)),
+            dma((RELAYED, 2)),
+            dma((RELAYED, 2)),
+            dma((RELAYED, 2)),
             dma((rows,)),
             dma((rows,)),
         ],
@@ -1039,7 +1086,7 @@
                 stencil_weights,
                 filter_mask,
                 cutoff_wave,
-                jnp.asarray(table),
+                jnp.asarray(whole_table.reshape(2, columns, 2 * KC)),
                 jnp.asarray(np.ascontiguousarray(table.T)),
             )
         )

time: 29.1 us -> 27.6 us (0.948)
  Pallas kernels: 28.8 us -> 27.5 us
    pallas_call x1, Pallas kernels: 26.4 us -> 25.1 us  [with_caps(): pl.pallas_call(caps_kernel, in_specs=[in_hbm] * 6, out_specs=in_vmem, out...]
where the time goes in v2:
time: 27.6 us; the launch traced here: 27.5 us
  Pallas kernels  27.5 us (100%)
    pallas_call x1, Pallas kernels, with_caps(): pl.pallas_call(caps_kernel, in_specs=[in_hbm] * 6, out_specs=in_vmem, out...  25.1 us
    pallas_call x1, Pallas kernels, with_caps(): pl.pallas_call(place_kernel, in_specs=[in_vmem], out_specs=in_hbm, out_sh...  2.42 us

profile of v2, /device:TPU:0, one launch (start us, length us, event | category | flops | bytes accessed | tf_op | source)
XLA Modules:
  0.0 27.5 jit_solution(5626163268106635384)
XLA Ops:
  0.0 25.1 %caps.1.stepped = f32[8,5,32,1024]{3,2,1,0:T(8,128)S(1)} custom-call(f32[5,32,8,1024]{3,2,1,0:T(8,128)} %state.1, f32[4,32,8,1024]{3,2,1,0:T(8,128)} %weights.1, s32[64]{0:T(128)} %mask_in.1, s32[64]{0:T(128)} %cutoff_in.1, bf16[2,1024,512]{2,1,0:T(8,128)(2,1)} %constant.4.clone.waves_in, bf16[512,1024]{1,0:T(8,128)(2,1)} %constant.5.clone.turned_in), custom_call_target="tpu_custom_call" | custom-call | tf_op jit(solution)/shard_map/caps/pallas_call | solution.py:1035
  25.1 2.4 %place.1 = f32[5,32,8,1024]{3,2,1,0:T(8,128)} custom-call(f32[8,5,32,1024]{3,2,1,0:T(8,128)S(1)} %caps.1.stepped), custom_call_target="tpu_custom_call" | custom-call | tf_op jit(solution)/shard_map/place/pallas_call | solution.py:1094

commit v3 on v2

--- a/solution.py
+++ b/solution.py
@@ -641,16 +641,13 @@
 
     @pl.when(polar)
     def _():
-        table_copies()[0].start()
+        for copy in table_copies():
+            copy.start()
 
     for copy in bound_copies():
         copy.start()
     for r in (*range(1, rows - 1), 0, rows - 1):
         weight_copy(r).start()
-
-    @pl.when(polar)
-    def _():
-        table_copies()[1].start()
 
     for r in (0, rows - 1):
         state_copy(r).wait()
@@ -887,6 +884,7 @@
     @pl.when(polar)
     def _():
         table_copies()[0].wait()
+        turn_back()
         odd_lines[...] = jnp.zeros_like(odd_lines)
 
         def two_rows(j, carry):
@@ -921,7 +919,6 @@
         combine_and_send(rows - 5)
         combine_and_send(rows - 4)
         combine_and_send(rows - 3)
-        turn_back()
 
     @pl.when(jnp.logical_not(polar))
     def _():
@@ -939,29 +936,35 @@
                 lend_copy(p, k).wait_recv()
                 pass_copy(p, k).start()
 
-    ready(0)
-    ready(rows - 1)
-    for field in range(fields):
-        for side, r in ((1, rows - 1), (0, 0)):
+    def edge_step(i, carry):
+        r = row_at(i)
+        side = jnp.where(r == 0, 0, 1)
+        ready(r)
+        for field in range(fields):
             edge_copy(0, field, side, (lat, across)).wait_recv()
             xs[side * (rows + 1), field] = halos[side, field].astype(jnp.float32)
             for group in range(groups):
                 advanced(r, field, group, *shares(r, group))
 
+        @pl.when(polar)
+        def _():
+            even_lines[...] = results[r].reshape(lines, columns).astype(jnp.bfloat16)
+            transform(even_lines, i)
+            half_copy(i).start()
+
+        return carry
+
+    lax.fori_loop(rows - 2, rows, edge_step, 0)
+
     @pl.when(polar)
     def _():
-        for i, lines_of in ((rows - 2, even_lines), (rows - 1, odd_lines)):
-            r = row_at(i)
-            lines_of[...] = results[r].reshape(lines, columns).astype(jnp.bfloat16)
-            transform(lines_of, i)
-            half_copy(i).start()
         def position(t):
             return jnp.where(t < 2 * RELAYED, t // 2 + RELAYED * (1 - lax.rem(t, 2)), t)
 
+        combine_and_send(rows - 2)
+        combine_and_send(rows - 1)
         finish(position(0))
         finish(position(1))
-        combine_and_send(rows - 2)
-        combine_and_send(rows - 1)
 
         def endings(t, carry):
             merge(position(t - 2))

time: 27.6 us -> 27.7 us (level)
  no operation moved by 1% of the time
where the time goes in v3:
time: 27.7 us; the launch traced here: 27.5 us
  Pallas kernels  27.5 us (99%)
    pallas_call x1, Pallas kernels, with_caps(): pl.pallas_call(caps_kernel, in_specs=[in_hbm] * 6, out_specs=in_vmem, out...  25.1 us
    pallas_call x1, Pallas kernels, with_caps(): pl.pallas_call(place_kernel, in_specs=[in_vmem], out_specs=in_hbm, out_sh...  2.42 us

profile of v3, /device:TPU:0, one launch (start us, length us, event | category | flops | bytes accessed | tf_op | source)
XLA Modules:
  0.0 27.5 jit_solution(17329039376806206924)
XLA Ops:
  0.0 25.1 %caps.1.stepped = f32[8,5,32,1024]{3,2,1,0:T(8,128)S(1)} custom-call(f32[5,32,8,1024]{3,2,1,0:T(8,128)} %state.1, f32[4,32,8,1024]{3,2,1,0:T(8,128)} %weights.1, s32[64]{0:T(128)} %mask_in.1, s32[64]{0:T(128)} %cutoff_in.1, bf16[2,1024,512]{2,1,0:T(8,128)(2,1)} %constant.4.clone.waves_in, bf16[512,1024]{1,0:T(8,128)(2,1)} %constant.5.clone.turned_in), custom_call_target="tpu_custom_call" | custom-call | tf_op jit(solution)/shard_map/caps/pallas_call | solution.py:1038
  25.1 2.4 %place.1 = f32[5,32,8,1024]{3,2,1,0:T(8,128)} custom-call(f32[8,5,32,1024]{3,2,1,0:T(8,128)S(1)} %caps.1.stepped), custom_call_target="tpu_custom_call" | custom-call | tf_op jit(solution)/shard_map/place/pallas_call | solution.py:1097

commit v4 on v3

--- a/solution.py
+++ b/solution.py
@@ -457,7 +457,7 @@
     return a.astype(jnp.bfloat16), b.astype(jnp.bfloat16)
 
 
-RELAYED = 3
+RELAYED = 2
 
 
 def caps_kernel(

time: 27.7 us -> 29.5 us (1.065)
  Pallas kernels: 27.5 us -> 29.3 us
    pallas_call x1, Pallas kernels: 25.1 us -> 26.9 us  [with_caps(): pl.pallas_call(caps_kernel, in_specs=[in_hbm] * 6, out_specs=in_vmem, out...]
where the time goes in v4:
time: 29.5 us; the launch traced here: 29.3 us
  Pallas kernels  29.3 us (99%)
    pallas_call x1, Pallas kernels, with_caps(): pl.pallas_call(caps_kernel, in_specs=[in_hbm] * 6, out_specs=in_vmem, out...  26.9 us
    pallas_call x1, Pallas kernels, with_caps(): pl.pallas_call(place_kernel, in_specs=[in_vmem], out_specs=in_hbm, out_sh...  2.42 us

profile of v4, /device:TPU:0, one launch (start us, length us, event | category | flops | bytes accessed | tf_op | source)
XLA Modules:
  0.0 29.3 jit_solution(13054095494001721697)
XLA Ops:
  0.0 26.9 %caps.1.stepped = f32[8,5,32,1024]{3,2,1,0:T(8,128)S(1)} custom-call(f32[5,32,8,1024]{3,2,1,0:T(8,128)} %state.1, f32[4,32,8,1024]{3,2,1,0:T(8,128)} %weights.1, s32[64]{0:T(128)} %mask_in.1, s32[64]{0:T(128)} %cutoff_in.1, bf16[2,1024,512]{2,1,0:T(8,128)(2,1)} %constant.4.clone.waves_in, bf16[512,1024]{1,0:T(8,128)(2,1)} %constant.5.clone.turned_in), custom_call_target="tpu_custom_call" | custom-call | tf_op jit(solution)/shard_map/caps/pallas_call | solution.py:1038
  26.9 2.4 %place.1 = f32[5,32,8,1024]{3,2,1,0:T(8,128)} custom-call(f32[8,5,32,1024]{3,2,1,0:T(8,128)S(1)} %caps.1.stepped), custom_call_target="tpu_custom_call" | custom-call | tf_op jit(solution)/shard_map/place/pallas_call | solution.py:1097
